TPU v7x, 32 devices: a whole 2x2x4 slice. The times are simulated.
32 devices in a mesh: ctx: 4 (over z), head: 8 (over y, x, core).
Axes of the slice: x: 2, y: 2, z: 4, core: 2. Of those that a mesh axis runs over, the one named last changes fastest.
Arguments:
- hidden: float32 [1024, 2304], P(('ctx', 'head')), may hold values from -40 to 40
- w_query: float32 [2304, 1536], P(None, 'head'), may hold values from -0.125 to 0.125
- w_down: float32 [2304, 576], replicated, may hold values from -0.125 to 0.125
- latent_gain: float32 [512], replicated, may hold values from 0.25 to 1.75
- w_key_up: float32 [512, 1024], P(None, 'head'), may hold values from -0.25 to 0.25
- w_value_up: float32 [512, 1024], P(None, 'head'), may hold values from -0.25 to 0.25
- w_out: float32 [1024, 2304], P('head'), may hold values from -0.1875 to 0.1875
Outputs:
- output: float32 [1024, 2304], P(('ctx', 'head'))
All inputs are finite; a program needn't handle non-finite values.
Results may differ from a plain program's by a relative error of at most 0.0003.
Values sent between devices are 32-bit elements; how exact they have to be, the bound alone decides.
A program may use at most 64 MiB of HBM per device.

v0:
```python
import jax
import jax.numpy as jnp
from jax import lax
from jax.sharding import PartitionSpec as P

EXACT = lax.Precision.HIGHEST
EPSILON = 1e-06
FLOOR = -1e30


def matmul(left, right):
    return jnp.dot(left, right, precision=EXACT, preferred_element_type=jnp.float32)


def on_device(hidden, w_query, w_down, latent_gain, w_key_up, w_value_up, w_out):
    rank = w_key_up.shape[0]
    nope = w_key_up.shape[1]
    down_part = matmul(hidden, w_down)
    raw_latent = down_part[:, :rank]
    meansq = jnp.mean(raw_latent * raw_latent, axis=-1, keepdims=True)
    own_latent = jnp.concatenate(
        [raw_latent * lax.rsqrt(meansq + EPSILON) * latent_gain, down_part[:, rank:]], axis=1
    )
    latent_block = lax.all_gather(own_latent, "head", axis=0, tiled=True)
    queries = matmul(lax.all_gather(hidden, "head", axis=0, tiled=True), w_query)
    row_count = queries.shape[0]
    score_scale = queries.shape[1] ** (-0.5)
    query_pos = lax.axis_index("ctx") * row_count + jnp.arange(row_count, dtype=jnp.int32)
    latent_part = latent_block[:, :rank]
    projected = jnp.concatenate(
        [matmul(latent_part, w_key_up), latent_block[:, rank:], matmul(latent_part, w_value_up)],
        axis=1,
    )
    shared_end = nope + latent_block.shape[1] - rank
    portion = lax.all_gather(projected, "ctx", axis=0, tiled=True)
    key_own = portion[:, :nope]
    maxima = jnp.full((row_count,), FLOOR, jnp.float32)
    scores = (
        matmul(queries[:, :nope], key_own.T)
        + matmul(queries[:, nope:], portion[:, nope:shared_end].T)
    ) * score_scale
    key_pos = jnp.arange(key_own.shape[0], dtype=jnp.int32)
    causal = query_pos[:, None] >= key_pos[None, :]
    scores = jnp.where(causal, scores, FLOOR)
    new_max = jnp.maximum(maxima, jnp.max(scores, axis=1))
    weights = jnp.where(causal, jnp.exp(scores - new_max[:, None]), 0.0)
    attended = matmul(weights, portion[:, shared_end:]) / jnp.sum(weights, axis=1)[:, None]
    return lax.psum_scatter(matmul(attended, w_out), "head", scatter_dimension=0, tiled=True)


def solution(mesh):
    placed = (
        P(("ctx", "head"), None),
        P(None, "head"),
        P(),
        P(),
        P(None, "head"),
        P(None, "head"),
        P("head", None),
    )
    return jax.shard_map(
        on_device, mesh=mesh, in_specs=placed, out_specs=P(("ctx", "head"), None), check_vma=False
    )
```

profile of v0, /device:TPU:0, one launch (start us, length us, event | category | flops | bytes accessed | tf_op | source)
XLA Modules:
  0.0 135.4 jit_solution(8996285080578068677)
XLA Ops:
  6.5 0.0 copy-start
  6.5 0.0 all-gather.3.cloned.1.call-start
  6.5 0.7 all-gather.3.cloned.1.call-update
  7.3 0.0 copy-start.4
  7.3 0.0 all-gather.5.cloned.1.call-start
  7.3 7.2 %fusion.19 = f32[32,576]{1,0:T(8,128)S(1)} fusion(f32[32,2304]{1,0:T(8,128)} %param.7, f32[2304,576]{0,1:T(8,128)} %param.9), kind=kOutput, calls=%fused_computation.30 | convolution fusion | flops 509607936 | bytes 5677056 | tf_op jit(solution)/shard_map/dot_general | solution.py:12
  14.5 0.0 copy-start.2
  14.5 0.0 copy-start.3
  14.5 0.1 multiply_reduce_fusion
  14.6 0.0 copy-done.4
  14.6 0.1 multiply_multiply_fusion
  14.7 13.6 %all_gather.10 = f32[256,576]{1,0:T(8,128)S(1)} all-gather(f32[32,576]{1,0:T(8,128)S(1)} %pad_maximum_fusion.1), channel_id=1, replica_groups=mesh['ctx'=4,'head'=8] {'head'}, dimensions={0}, use_global_device_ids=true | all-gather | bytes 663552 | tf_op jit(solution)/shard_map/all_gather | solution.py:24
  28.3 0.1 copy.8
  28.4 0.0 copy-done.2
  28.4 0.6 fusion.8
  29.0 0.0 copy-done.3
  29.0 0.6 fusion.10
  29.6 0.7 pad_maximum_fusion
  30.4 0.0 all-gather.5.cloned.1.call-update
  30.4 0.2 reduce-scatter.2.cloned.1.call-start
  30.6 12.1 %all-gather.3.cloned.1.call-done = f32[256,2304]{1,0:T(8,128)} async-done(((f32[32,2304]{1,0:T(8,128)}), f32[256,2304]{1,0:T(8,128)}) %all-gather.3.cloned.1.call-update) | async-done | bytes 2359312 | tf_op jit(solution)/shard_map/all_gather | solution.py:25
  42.7 0.0 copy-done
  42.7 4.1 %fusion.18 = f32[256,192]{0,1:T(8,128)S(1)} fusion(f32[256,2304]{1,0:T(8,128)} %all-gather.3.cloned.1.call-done, f32[2304,192]{0,1:T(8,128)S(1)} %copy-done), kind=kOutput, calls=%fused_computation.29 | convolution fusion | flops 1358954496 | bytes 4325376 | tf_op jit(solution)/shard_map/dot_general | solution.py:12
  46.9 30.0 %all-gather.5.cloned.1.call-done = f32[1024,320]{0,1:T(8,128)} async-done(((f32[256,320]{0,1:T(8,128)}), f32[1024,320]{0,1:T(8,128)}) %all-gather.5.cloned.1.call-update) | async-done | bytes 1310736 | tf_op jit(solution)/shard_map/all_gather | solution.py:35
  76.9 2.0 %fusion.12 = f32[256,1024]{1,0:T(8,128)S(1)} fusion(f32[1024,320]{0,1:T(8,128)} %all-gather.5.cloned.1.call-done, f32[256,192]{0,1:T(8,128)S(1)} %fusion.18), kind=kOutput, calls=%fused_computation.17 | convolution fusion | flops 201326592 | bytes 1376256 | tf_op jit(solution)/shard_map/dot_general | solution.py:12
  78.8 2.3 %fusion.17 = (f32[256]{0:T(256)S(1)}, f32[256,1024]{1,0:T(8,128)S(1)}) fusion(f32[256,1024]{1,0:T(8,128)S(1)} %fusion.12, f32[1024,320]{0,1:T(8,128)} %all-gather.5.cloned.1.call-done, f32[256,192]{0,1:T(8,128)S(1)} %fusion.18, s32[256]{0:T(256)S(1)} %iota_add_fusion), kind=kOutput, calls=%fused_computation.28 | convolution fusion | flops 403963648 | bytes 2754560 | tf_op jit(solution)/shard_map/dot_general | solution.py:12
  81.1 0.0 copy-start.1
  81.2 0.4 fusion.2
  81.6 2.2 %convolution_divide_fusion = f32[256,128]{1,0:T(8,128)S(1)} fusion(f32[256,1024]{1,0:T(8,128)S(1)} %get-tuple-element.6, f32[1024,320]{0,1:T(8,128)} %all-gather.5.cloned.1.call-done, f32[256]{0:T(256)S(1)} %broadcast_maximum_fusion, s32[256]{0:T(256)S(1)} %iota_add_fusion, f32[256]{0:T(256)S(1)} %fusion.2), kind=kOutput, calls=%fused_computation.3 | convolution fusion | flops 403472384 | bytes 1707008 | tf_op jit(solution)/shard_map/dot_general | solution.py:12
  83.8 0.0 copy-done.1
  83.8 3.4 %fusion.20 = f32[256,2304]{1,0:T(8,128)} fusion(f32[256,128]{1,0:T(8,128)S(1)} %convolution_divide_fusion, f32[128,2304]{1,0:T(8,128)S(1)} %copy-done.1), kind=kOutput, calls=%fused_computation.31 | convolution fusion | flops 905969664 | bytes 3670016 | tf_op jit(solution)/shard_map/dot_general | solution.py:12
  87.2 0.0 reduce-scatter.2.cloned.1.call-update
  87.3 41.6 %reduce-scatter.2.cloned.1.call-done = f32[32,2304]{1,0:T(8,128)} async-done(((f32[256,2304]{1,0:T(8,128)}), f32[32,2304]{1,0:T(8,128)}) %reduce-scatter.2.cloned.1.call-update) | async-done | bytes 294928 | tf_op jit(solution)/shard_map/reduce_scatter | solution.py:48
  (6 shorter events, 0.0 us)
Async XLA Ops:
  6.5 36.2 %copy-start = (f32[2304,192]{0,1:T(8,128)S(1)}, f32[2304,192]{0,1:T(8,128)}, u32[]{:S(2)}) copy-start(f32[2304,192]{0,1:T(8,128)} %param.8) | copy-start | bytes 5308420
  6.5 36.2 %all-gather.3.cloned.1.call-start = ((), (), s32[]{:S(2)}) async-start(), calls=%async_computation.1 | async-start | bytes 2654208 | tf_op jit(solution)/shard_map/all_gather | solution.py:25
  7.3 7.4 %copy-start.4 = (f32[512]{0:T(512)S(1)}, f32[512]{0:T(512)}, u32[]{:S(2)}) copy-start(f32[512]{0:T(512)} %param.10) | copy-start | bytes 6148
  7.3 69.6 %all-gather.5.cloned.1.call-start = ((), (), s32[]{:S(2)}) async-start(), calls=%async_computation.2 | async-start | bytes 1638400 | tf_op jit(solution)/shard_map/all_gather | solution.py:35
  14.5 13.9 %copy-start.2 = (f32[512,128]{1,0:T(8,128)S(1)}, f32[512,128]{1,0:T(8,128)}, u32[]{:S(2)}) copy-start(f32[512,128]{1,0:T(8,128)} %param.12) | copy-start | bytes 786436
  14.5 14.5 %copy-start.3 = (f32[512,128]{1,0:T(8,128)S(1)}, f32[512,128]{1,0:T(8,128)}, u32[]{:S(2)}) copy-start(f32[512,128]{1,0:T(8,128)} %param.11) | copy-start | bytes 786436
  30.4 98.5 %reduce-scatter.2.cloned.1.call-start = ((), (), s32[]{:S(2)}) async-start(), calls=%async_computation.3 | async-start | bytes 2654208 | tf_op jit(solution)/shard_map/reduce_scatter | solution.py:48
  81.1 2.6 %copy-start.1 = (f32[128,2304]{1,0:T(8,128)S(1)}, f32[128,2304]{1,0:T(8,128)}, u32[]{:S(2)}) copy-start(f32[128,2304]{1,0:T(8,128)} %param.13) | copy-start | bytes 3538948
Sparse Core Ops, SparseCore 0:
  9.2 33.4 all-gather.2
  44.3 32.5 all-gather.4
  87.4 41.4 reduce-scatter.1
where the time goes:
time: 136 us; the launch traced here: 135 us
  waiting for transfers between devices  84.5 us (62%)
  matrix products  22.4 us (16%)
  blocking collectives  13.6 us (10%)
  between operations  13.3 us (10%)
    reduce_scatter x1, waiting for transfers between devices, on_device(): lax.psum_scatter(matmul(attended, w_out), 'head', scatter_dimension=0, ti...  41.6 us
    all_gather x1, waiting for transfers between devices, on_device(): portion = lax.all_gather(projected, 'ctx', axis=0, tiled=True)  30 us
    dot_general x8, matrix products, matmul(): jnp.dot(left, right, precision=EXACT, preferred_element_type=jnp.float32)  22.4 us
    all_gather x1, blocking collectives, on_device(): latent_block = lax.all_gather(own_latent, 'head', axis=0, tiled=True)  13.6 us
    all_gather x1, waiting for transfers between devices, on_device(): lax.all_gather(hidden, 'head', axis=0, tiled=True)  12.1 us
  transfers between devices with their start and end apart: 3, of which 3 were waited for; matrix products, arithmetic and copies ran while one was open for 10% of the time, Pallas kernels for 0%

commit v1 on v0

--- a/solution.py
+++ b/solution.py
@@ -32,7 +32,14 @@
         axis=1,
     )
     shared_end = nope + latent_block.shape[1] - rank
-    portion = lax.all_gather(projected, "ctx", axis=0, tiled=True)
+    count = lax.axis_size("ctx")
+    route = [(i, (i + 1) % count) for i in range(count)]
+    terms = [projected]
+    for reach in range(1, count):
+        terms = [lax.ppermute(terms[0], "ctx", route), *terms]
+    whole = jnp.concatenate(terms, axis=0)
+    turn = (lax.axis_index("ctx") + 1) * terms[-1].shape[0]
+    portion = jnp.roll(whole, turn, axis=0)
     key_own = portion[:, :nope]
     maxima = jnp.full((row_count,), FLOOR, jnp.float32)
     scores = (

time: 136 us -> 130 us (0.956)
  waiting for transfers between devices: 84.5 us -> 71.6 us
  local copies, waits for them, and re-layouts: 0.12 us -> 4.94 us
  starting transfers between devices: 0.26 us -> 1.67 us
    ppermute x0 -> x3, waiting for transfers between devices: none -> 31.1 us  [on_device(): terms = [lax.ppermute(terms[0], 'ctx', route), *terms]]
    all_gather x1 -> x0, waiting for transfers between devices: 30 us -> none  [on_device(): portion = lax.all_gather(projected, 'ctx', axis=0, tiled=True)]
    all_gather x1, waiting for transfers between devices: 12.1 us -> 0.01 us  [on_device(): lax.all_gather(hidden, 'head', axis=0, tiled=True)]
    unnamed x10 -> x16, local copies, waits for them, and re-layouts: 0.02 us -> 4.85 us
    reduce_scatter x1, waiting for transfers between devices: 41.6 us -> 39.7 us  [on_device(): lax.psum_scatter(matmul(attended, w_out), 'head', scatter_dimension=0, ti...]
    ppermute x0 -> x3, starting transfers between devices: none -> 1.63 us  [on_device(): terms = [lax.ppermute(terms[0], 'ctx', route), *terms]]
  transfers between devices with their start and end apart: 3 -> 5, of which waited for: 3 -> 4; matrix products, arithmetic and copies ran while one was open for 10% -> 12% of each run, Pallas kernels for 0% -> 0%
where the time goes in v1:
time: 130 us
  waiting for transfers between devices  71.6 us (55%)
  matrix products  22.5 us (17%)
  blocking collectives  13.6 us (10%)
  between operations  13.5 us (10%)
  local copies, waits for them, and re-layouts  4.94 us (4%)
  other arithmetic  2.24 us (2%)
  starting transfers between devices  1.67 us (1%)
    reduce_scatter x1, waiting for transfers between devices, on_device(): lax.psum_scatter(matmul(attended, w_out), 'head', scatter_dimension=0, ti...  39.7 us
    ppermute x3, waiting for transfers between devices, on_device(): terms = [lax.ppermute(terms[0], 'ctx', route), *terms]  31.1 us
    dot_general x8, matrix products, matmul(): jnp.dot(left, right, precision=EXACT, preferred_element_type=jnp.float32)  22.5 us
    all_gather x1, blocking collectives, on_device(): latent_block = lax.all_gather(own_latent, 'head', axis=0, tiled=True)  13.6 us
    unnamed x16, local copies, waits for them, and re-layouts  4.85 us
  transfers between devices with their start and end apart: 5, of which 4 were waited for; matrix products, arithmetic and copies ran while one was open for 12% of the time, Pallas kernels for 0%

profile of v1, /device:TPU:0, one launch (start us, length us, event | category | flops | bytes accessed | tf_op | source)
XLA Modules:
  0.0 130.1 jit_solution(6857529045695230183)
XLA Ops:
  6.5 0.0 copy-start
  6.5 0.0 all-gather.2.cloned.1.call-start
  6.5 0.7 all-gather.2.cloned.1.call-update
  7.3 0.0 copy-start.4
  7.3 0.0 copy-start.2
  7.3 0.0 reduce-scatter.2.cloned.1.call-start
  7.3 7.2 %fusion.20 = f32[32,576]{1,0:T(8,128)S(1)} fusion(f32[32,2304]{1,0:T(8,128)} %param.7, f32[2304,576]{0,1:T(8,128)} %param.9), kind=kOutput, calls=%fused_computation.39 | convolution fusion | flops 509607936 | bytes 5677056 | tf_op jit(solution)/shard_map/dot_general | solution.py:12
  14.5 0.0 copy-start.3
  14.5 0.1 multiply_reduce_fusion
  14.7 0.0 copy-done.4
  14.7 0.1 multiply_multiply_fusion
  14.8 13.6 %all_gather.7 = f32[256,576]{1,0:T(8,128)S(1)} all-gather(f32[32,576]{1,0:T(8,128)S(1)} %pad_maximum_fusion.1), channel_id=1, replica_groups=mesh['ctx'=4,'head'=8] {'head'}, dimensions={0}, use_global_device_ids=true | all-gather | bytes 663552 | tf_op jit(solution)/shard_map/all_gather | solution.py:24
  28.3 0.1 copy.8
  28.4 0.0 copy-done.2
  28.4 0.6 fusion.10
  29.0 0.0 copy-done.3
  29.0 0.6 fusion.8
  29.7 1.6 %collective-permute-start = (f32[256,320]{0,1:T(8,128)S(1)}, f32[256,320]{0,1:T(8,128)S(1)}, u32[]{:S(2)}, u32[]{:S(2)}) collective-permute-start(f32[256,320]{0,1:T(8,128)S(1)} %pad_maximum_fusion), channel_id=1, source_target_pairs={{0,8},{8,16},{16,24},{24,0},{1,9},{9,17},{17,25},{25,1},{2,10},{10... | collective-permute-start | bytes 983048 | tf_op jit(solution)/shard_map/ppermute | solution.py:39
  31.3 10.2 %collective-permute-done = f32[256,320]{0,1:T(8,128)S(1)} collective-permute-done((f32[256,320]{0,1:T(8,128)S(1)}, f32[256,320]{0,1:T(8,128)S(1)}, u32[]{:S(2)}, u32[]{:S(2)}) %collective-permute-start) | collective-permute-done | bytes 327712 | tf_op jit(solution)/shard_map/ppermute | solution.py:39
  41.5 0.0 collective-permute-start.1
  41.5 10.9 %collective-permute-done.1 = f32[256,320]{0,1:T(8,128)S(1)} collective-permute-done((f32[256,320]{0,1:T(8,128)S(1)}, f32[256,320]{0,1:T(8,128)S(1)}, u32[]{:S(2)}, u32[]{:S(2)}) %collective-permute-start.1) | collective-permute-done | bytes 327712 | tf_op jit(solution)/shard_map/ppermute | solution.py:39
  52.4 0.0 collective-permute-start.2
  52.4 10.0 %collective-permute-done.2 = f32[256,320]{0,1:T(8,128)S(1)} collective-permute-done((f32[256,320]{0,1:T(8,128)S(1)}, f32[256,320]{0,1:T(8,128)S(1)}, u32[]{:S(2)}, u32[]{:S(2)}) %collective-permute-start.2) | collective-permute-done | bytes 327712 | tf_op jit(solution)/shard_map/ppermute | solution.py:39
  62.5 0.8 constant_dynamic-update-slice_fusion.7
  63.3 0.8 constant_dynamic-update-slice_fusion.6
  64.1 0.8 constant_dynamic-update-slice_fusion.5
  64.9 0.8 constant_dynamic-update-slice_fusion.4
  65.7 0.8 constant_dynamic-update-slice_fusion.3
  66.5 0.8 constant_dynamic-update-slice_fusion.2
  67.3 0.8 constant_dynamic-update-slice_fusion.1
  68.1 0.8 constant_dynamic-update-slice_fusion
  68.9 0.0 all-gather.2.cloned.1.call-done
  68.9 0.0 copy-done
  68.9 4.1 %fusion.19 = f32[256,192]{0,1:T(8,128)S(1)} fusion(f32[256,2304]{1,0:T(8,128)} %all-gather.2.cloned.1.call-done, f32[2304,192]{0,1:T(8,128)S(1)} %copy-done), kind=kOutput, calls=%fused_computation.38 | convolution fusion | flops 1358954496 | bytes 4325376 | tf_op jit(solution)/shard_map/dot_general | solution.py:12
  73.0 2.0 %fusion.12 = f32[256,1024]{1,0:T(8,128)S(1)} fusion(f32[2048,320]{0,1:T(8,128)} %constant_dynamic-update-slice_fusion, s32[]{:T(128)S(6)} %select_n.21, s32[]{:T(128)S(6)} %add.47, f32[256,192]{0,1:T(8,128)S(1)} %fusion.19), kind=kOutput, calls=%fused_computation.17 | convolution fusion | flops 201326592 | bytes 1376264 | tf_op jit(solution)/shard_map/dot_general | solution.py:12
  75.0 0.0 copy-start.1
  75.0 2.4 %fusion.18 = (f32[256]{0:T(256)S(1)}, f32[256,1024]{1,0:T(8,128)S(1)}) fusion(f32[256,1024]{1,0:T(8,128)S(1)} %fusion.12, f32[2048,320]{0,1:T(8,128)} %constant_dynamic-update-slice_fusion, s32[]{:T(128)S(6)} %select_n.21, f32[256,192]{0,1:T(8,128)S(1)} %fusion.19, s32[256]{0:T(256)S(1)} %iota_add_fusion), kind=kOutput, calls=%fused_computation.37 | convolution fusion | flops 403963648 | bytes 2754564 | tf_op jit(solution)/shard_map/dot_general | solution.py:12
  77.4 0.4 fusion.2
  77.8 2.2 %convolution_divide_fusion = f32[256,128]{1,0:T(8,128)S(1)} fusion(f32[256,1024]{1,0:T(8,128)S(1)} %get-tuple-element.6, f32[2048,320]{0,1:T(8,128)} %constant_dynamic-update-slice_fusion, s32[]{:T(128)S(6)} %select_n.21, s32[]{:T(128)S(6)} %add.48, f32[256]{0:T(256)S(1)} %broadcast_maximum_fusion, s32[256]{0:T(256)S(1)} %iota_add_fusion, f32[256]{0:T(256)S(1)} %fusion.2), kind=kOutput, calls=%fused_computation.3 | convolution fusion | flops 403472384 | bytes 1707016 | tf_op jit(solution)/shard_map/dot_general | solution.py:12
  80.1 0.0 copy-done.1
  80.1 3.4 %fusion.21 = f32[256,2304]{1,0:T(8,128)} fusion(f32[256,128]{1,0:T(8,128)S(1)} %convolution_divide_fusion, f32[128,2304]{1,0:T(8,128)S(1)} %copy-done.1), kind=kOutput, calls=%fused_computation.40 | convolution fusion | flops 905969664 | bytes 3670016 | tf_op jit(solution)/shard_map/dot_general | solution.py:12
  83.5 0.0 reduce-scatter.2.cloned.1.call-update
  83.5 39.7 %reduce-scatter.2.cloned.1.call-done = f32[32,2304]{1,0:T(8,128)} async-done(((f32[256,2304]{1,0:T(8,128)}), f32[32,2304]{1,0:T(8,128)}) %reduce-scatter.2.cloned.1.call-update) | async-done | bytes 294928 | tf_op jit(solution)/shard_map/reduce_scatter | solution.py:55
  (7 shorter events, 0.1 us)
Async XLA Ops:
  6.5 62.4 %copy-start = (f32[2304,192]{0,1:T(8,128)S(1)}, f32[2304,192]{0,1:T(8,128)}, u32[]{:S(2)}) copy-start(f32[2304,192]{0,1:T(8,128)} %param.8) | copy-start | bytes 5308420
  6.5 62.3 %all-gather.2.cloned.1.call-start = ((), (), s32[]{:S(2)}) async-start(), calls=%async_computation.1 | async-start | bytes 2654208 | tf_op jit(solution)/shard_map/all_gather | solution.py:25
  7.3 7.4 %copy-start.4 = (f32[512]{0:T(512)S(1)}, f32[512]{0:T(512)}, u32[]{:S(2)}) copy-start(f32[512]{0:T(512)} %param.10) | copy-start | bytes 6148
  7.3 21.2 %copy-start.2 = (f32[512,128]{1,0:T(8,128)S(1)}, f32[512,128]{1,0:T(8,128)}, u32[]{:S(2)}) copy-start(f32[512,128]{1,0:T(8,128)} %param.11) | copy-start | bytes 786436
  7.3 116.0 %reduce-scatter.2.cloned.1.call-start = ((), (), s32[]{:S(2)}) async-start(), calls=%async_computation.2 | async-start | bytes 2654208 | tf_op jit(solution)/shard_map/reduce_scatter | solution.py:55
  14.5 14.5 %copy-start.3 = (f32[512,128]{1,0:T(8,128)S(1)}, f32[512,128]{1,0:T(8,128)}, u32[]{:S(2)}) copy-start(f32[512,128]{1,0:T(8,128)} %param.12) | copy-start | bytes 786436
  29.7 11.8 %collective-permute-start = (f32[256,320]{0,1:T(8,128)S(1)}, f32[256,320]{0,1:T(8,128)S(1)}, u32[]{:S(2)}, u32[]{:S(2)}) collective-permute-start(f32[256,320]{0,1:T(8,128)S(1)} %pad_maximum_fusion), channel_id=1, source_target_pairs={{0,8},{8,16},{16,24},{24,0},{1,9},{9,17},{17,25},{25,1},{2,10},{10... | collective-permute-start | bytes 983048 | tf_op jit(solution)/shard_map/ppermute | solution.py:39
  41.5 10.9 %collective-permute-start.1 = (f32[256,320]{0,1:T(8,128)S(1)}, f32[256,320]{0,1:T(8,128)S(1)}, u32[]{:S(2)}, u32[]{:S(2)}) collective-permute-start(f32[256,320]{0,1:T(8,128)S(1)} %collective-permute-done), channel_id=1, source_target_pairs={{0,8},{8,16},{16,24},{24,0},{1,9},{9,17},{17,25},{25,1},{2,10},{10... | collective-permute-start | bytes 983048 | tf_op jit(solution)/shard_map/ppermute | solution.py:39
  52.4 10.1 %collective-permute-start.2 = (f32[256,320]{0,1:T(8,128)S(1)}, f32[256,320]{0,1:T(8,128)S(1)}, u32[]{:S(2)}, u32[]{:S(2)}) collective-permute-start(f32[256,320]{0,1:T(8,128)S(1)} %collective-permute-done.1), channel_id=1, source_target_pairs={{0,8},{8,16},{16,24},{24,0},{1,9},{9,17},{17,25},{25,1},{2,10},{10... | collective-permute-start | bytes 983048 | tf_op jit(solution)/shard_map/ppermute | solution.py:39
  75.0 5.1 %copy-start.1 = (f32[128,2304]{1,0:T(8,128)S(1)}, f32[128,2304]{1,0:T(8,128)}, u32[]{:S(2)}) copy-start(f32[128,2304]{1,0:T(8,128)} %param.13) | copy-start | bytes 3538948
Sparse Core Ops, SparseCore 0:
  9.2 33.4 all-gather.1
  83.7 39.5 reduce-scatter.1
